TPU v7x, 256 devices: a whole 4x4x8 slice. The times are simulated.
256 devices in a mesh: tm: 8 (over y, z_hi), lat: 32 (over x, z_lo, core).
Axes of the slice: x: 4, y: 4, z: 8 (z_hi: 2, z_lo: 4; z = z_hi * 4 + z_lo), core: 2. Of those that a mesh axis runs over, the one named last changes fastest.
Arguments:
- background: bfloat16 [16, 2, 512, 2048], P('tm', None, 'lat'), may hold values from -12 to 12
- conv_weight: bfloat16 [32, 90], replicated, may hold values from -0.625 to 0.625
- conv_bias: float32 [32], replicated, may hold values from -3 to 3
- mix_weight: bfloat16 [32, 32], replicated, may hold values from -1 to 1
- mix_bias: float32 [32], replicated, may hold values from -3 to 3
- out_weight: bfloat16 [2, 32], replicated, may hold values from -0.1875 to 0.1875
- out_bias: float32 [2], replicated, may hold values from -0.3 to 0.3
- drift_east: float32 [512, 2048], P('lat', 'tm'), may hold values from -0.2 to 0.2
- drift_north: float32 [512, 2048], P('lat', 'tm'), may hold values from -0.2 to 0.2
- diffusivity: float32 [512, 2048], P('lat', 'tm'), may hold values from 0.1 to 0.24
- sensors: int32 [16, 32, 8, 128], P(None, 'lat', 'tm'), may hold values from 0 to 4095, as said below
- observations: float32 [16, 32, 8, 2, 128], P(None, 'lat', 'tm'), may hold values from -6 to 6
Outputs:
- total_score: float32 [16, 2, 512, 2048], P('tm', None, 'lat')
Inputs may be any that keep to these rules, and one draw needn't show every extreme that they name: `sensors`: each entry is a cell of its tile counted row by row over 16 rows of 256 cells; cells may repeat.
All inputs are finite; a program needn't handle non-finite values.
Results may differ from a plain program's by a relative error of at most 0.0039.
Values may be sent and summed in bfloat16 or wider, within the bound.
A program may use at most 128 MiB of HBM per device.

v0:
```python
import functools

import jax
import jax.numpy as jnp
from jax import lax
from jax.experimental import pallas as pl
from jax.experimental.pallas import tpu as pltpu
from jax.sharding import PartitionSpec as P

MESH = pl.DeviceIdType.MESH
F32, BF16, I32 = jnp.float32, jnp.bfloat16, jnp.int32
N_TM = 8
ROWS, LON, TILE = 16, 2048, 256
HID, TAPS, KT, SUB = 32, 90, 5, 3
MID_K = 0.17
CHUNKS = 8
WIDTH = LON // CHUNKS
GELU_A = 1.5957691216057308
GELU_B = 0.2854192627
MAIN, EXTRA = 160, 32
KDIM = MAIN + EXTRA


def gelu_of_twice(y):
    t = jnp.tanh(y * (GELU_A + GELU_B * (y * y)))
    return (y + y * t).astype(BF16)


def iota(shape, dim):
    return lax.broadcasted_iota(I32, shape, dim)


def as_f32(mask):
    return jnp.where(mask, 1.0, 0.0).astype(F32)


def column(row):
    n = row.shape[1]
    eye = iota((n, n), 0) == iota((n, n), 1)
    return jnp.sum(jnp.where(eye, jnp.broadcast_to(row, (n, n)), 0.0), axis=1, keepdims=True)


def build_weights(tm, lat, n_lat, cw, cb, mw, mb, ow, w_sc, mix_sc, mixb_sc, out_sc):
    half_cw = (cw[...].astype(F32) * 0.5).astype(BF16)
    bias = column(cb[...] * 0.5)
    bias_hi = bias.astype(BF16).astype(F32)
    bias_lo = bias - bias_hi
    k = iota((1, KDIM), 1)
    main = k < MAIN
    kk = k - MAIN
    group_h, edge, f_h = kk // 8, (kk // 4) % 2, (kk // 2) % 2
    c = jnp.where(main, (k // 16) % 2, kk % 2)
    row_in = k % 16
    has_prev, has_next = tm > 0, tm < N_TM - 1
    has_south, has_north = lat > 0, lat < n_lat - 1
    bias_row = jnp.where(k == MAIN + 24, 1.0, 0.0).astype(F32) * bias_hi + jnp.where(k == MAIN + 25, 1.0, 0.0).astype(F32) * bias_lo
    expanded = {}
    for t in range(2):
        lag = jnp.where(main, k // 32, 2 * group_h + f_h - t)
        group = (lag + t) // 2
        ok = (lag >= 0) & (lag < KT) & (main | (kk < 24))
        ok = ok & ((group > 0) | has_prev) & ((group < 2) | has_next)
        for j in range(3):
            for i in range(3):
                tap = jnp.where(ok, ((c * KT + lag) * 3 + i) * 3 + j, -1)
                select = as_f32(iota((TAPS, KDIM), 0) == tap).astype(BF16)
                expanded[t, j, i] = jnp.dot(half_cw, select, preferred_element_type=F32)

    def one_row(r, carry):
        spot = [as_f32(main & (row_in == r + i - 1)) for i in range(3)]
        spot[0] = spot[0] + as_f32((~main) & (edge == 0) & (r == 0) & has_south)
        spot[2] = spot[2] + as_f32((~main) & (edge == 1) & (r == ROWS - 1) & has_north)
        for t in range(2):
            for j in range(3):
                val = expanded[t, j, 0] * spot[0] + expanded[t, j, 1] * spot[1] + expanded[t, j, 2] * spot[2]
                if j == 1:
                    val = val + bias_row
                w_sc[t, j, pl.ds(pl.multiple_of(r * HID, HID), HID), :] = val.astype(BF16)
        return carry

    lax.fori_loop(0, ROWS, one_row, 0)
    spread_lanes = as_f32(iota((HID, 8 * HID), 1) % HID == iota((HID, 8 * HID), 0)).astype(BF16)
    lane_row = iota((1, 8 * HID), 1) // HID
    mix_wide = jnp.dot((mw[...].astype(F32) * 0.5).astype(BF16), spread_lanes, preferred_element_type=F32)
    for r in range(8):
        mix_sc[r * HID:(r + 1) * HID, :] = (mix_wide * as_f32(lane_row == r)).astype(BF16)
    mixb_sc[...] = jnp.broadcast_to(column(mb[...] * 0.5), (HID, WIDTH))
    out_wide = jnp.dot(ow[...], spread_lanes, preferred_element_type=F32)
    own_row = iota((16, 8 * HID), 1) // HID == iota((16, 8 * HID), 0) % 8
    first_var = iota((16, 8 * HID), 0) < 8
    both = jnp.where(first_var, jnp.broadcast_to(out_wide[0:1], (16, 8 * HID)), jnp.broadcast_to(out_wide[1:2], (16, 8 * HID)))
    out_sc[...] = jnp.where(own_row, both, 0.0).astype(BF16)


def build_edges(h_sc, hx_sc):
    half = LON // 2
    for hf in range(2):
        parts = []
        for g in range(3):
            for e in range(2):
                parts.append(h_sc[g, e].astype(F32)[hf * 4:hf * 4 + 4, :])
        tail = as_f32(iota((8, half), 0) < 2)
        hx_sc[:, hf * half:(hf + 1) * half] = jnp.concatenate(parts + [tail], axis=0).astype(BF16)


def build_coefficients(lat, n_lat, call_sc, cf_sc):
    for q in range(4):
        live = 1.0
        if q == 0:
            live = jnp.where(lat > 0, 1.0, 0.0).astype(F32)
        if q == 3:
            live = jnp.where(lat < n_lat - 1, 1.0, 0.0).astype(F32)
        for tile in range(N_TM):
            a = call_sc[tile, q, 0].astype(F32) * 0.5
            b = call_sc[tile, q, 1].astype(F32) * 0.5
            k = call_sc[tile, q, 2].astype(F32) + MID_K
            rows, lanes = slice(q * 8, q * 8 + 8), slice(tile * TILE, (tile + 1) * TILE)
            cf_sc[0, rows, lanes] = (1.0 - 4.0 * k) * live
            cf_sc[1, rows, lanes] = (k - a) * live
            cf_sc[2, rows, lanes] = (k + a) * live
            cf_sc[3, rows, lanes] = (k - b) * live
            cf_sc[4, rows, lanes] = (k + b) * live


def build_spread(sens_sc, obs_sc, cnt_sc, os_sc):
    row = iota((32, 128), 0)
    col = iota((TILE, 128), 0)

    def one(n, carry):
        tile, f = n // 2, n % 2
        lanes = pl.ds(pl.multiple_of(tile * TILE, TILE), TILE)
        left, right = [], []
        for side in range(3):
            cell = sens_sc[side, tile, f, 0]
            there = cell // TILE + (side * 16 - 8)
            pick = as_f32(jnp.broadcast_to(there, (32, 128)) == row)
            value = obs_sc[side, tile, f, 0, 0]
            high = value.astype(BF16).astype(F32)
            low = value - high
            left.append(jnp.concatenate([pick, pick * high[0:1], pick * high[1:2], pick * low[0:1], pick * low[1:2]], axis=0).astype(BF16))
            right.append(as_f32(jnp.broadcast_to(cell % TILE, (TILE, 128)) == col).astype(BF16))
        total = jnp.zeros((160, TILE), F32)
        for side in range(3):
            total = total + lax.dot_general(left[side], right[side], (((1,), (1,)), ((), ())), preferred_element_type=F32)
        cnt_sc[f, :, lanes] = total[0:32]
        os_sc[f, 0, :, lanes] = total[32:64] + total[96:128]
        os_sc[f, 1, :, lanes] = total[64:96] + total[128:160]
        return carry

    lax.fori_loop(0, 2 * N_TM, one, 0)


def likelihood(lat, n_lat, xg_sc, halo_sc, cf_sc, cnt_sc, os_sc, adj_sc):
    south = jnp.where(lat > 0, 1.0, 0.0).astype(F32)
    north = jnp.where(lat < n_lat - 1, 1.0, 0.0).astype(F32)

    def one(n, carry):
        f, c = n // 2, n % 2
        u = jnp.concatenate([halo_sc[0, f, c].astype(F32) * south, xg_sc[1, f, c].astype(F32), halo_sc[1, f, c].astype(F32) * north], axis=0)
        for _ in range(SUB):
            u = (cf_sc[0] * u + cf_sc[1] * pltpu.roll(u, LON - 1, 1) + cf_sc[2] * pltpu.roll(u, 1, 1)
                 + cf_sc[3] * pltpu.roll(u, 31, 0) + cf_sc[4] * pltpu.roll(u, 1, 0))
        v = cnt_sc[f] * u - os_sc[f, c]
        for _ in range(SUB):
            v = (cf_sc[0] * v + pltpu.roll(cf_sc[1] * v, 1, 1) + pltpu.roll(cf_sc[2] * v, LON - 1, 1)
                 + pltpu.roll(cf_sc[3] * v, 1, 0) + pltpu.roll(cf_sc[4] * v, 31, 0))
        adj_sc[f, c] = v[8:24]
        return carry

    lax.fori_loop(0, 4, one, 0)


def score_chunk(n, xg_sc, hx_sc, rh_sc, w_sc, mix_sc, mixb_sc, out_sc, ob, adj_sc, out):
    base = pl.multiple_of(n * WIDTH, WIDTH)
    before = pl.multiple_of(lax.rem(n * WIDTH + LON - 128, LON), 128)
    after = pl.multiple_of(lax.rem(n * WIDTH + WIDTH, LON), 128)
    here = pl.ds(base, WIDTH)
    for piece in range(14):
        if piece < 12:
            g, f, c = piece // 4, (piece // 2) % 2, piece % 2
            load = lambda lanes: xg_sc[g, f, c, :, lanes]
        else:
            load = lambda lanes: hx_sc[(piece - 12) * 16:(piece - 11) * 16, lanes]
        rows = slice(piece * 16, piece * 16 + 16)
        mid = load(here)
        prev, nxt = load(pl.ds(before, 128)), load(pl.ds(after, 128))
        rh_sc[0, rows, :] = shift_lanes(jnp.concatenate([prev, mid], axis=1), 1)[:, 128:]
        rh_sc[1, rows, :] = mid
        rh_sc[2, rows, :] = shift_lanes(jnp.concatenate([mid, nxt], axis=1), WIDTH + 127)[:, :WIDTH]
    for t in range(2):
        y = None
        for j in range(3):
            rhs = jnp.concatenate([rh_sc[j, t * 32:t * 32 + MAIN, :], rh_sc[j, 192:224, :]], axis=0)
            part = jnp.dot(w_sc[t, j], rhs, preferred_element_type=F32)
            y = part if y is None else y + part
        first = gelu_of_twice(y)
        for rb in range(2):
            z = jnp.dot(mix_sc[...], first[rb * 256:(rb + 1) * 256], preferred_element_type=F32)
            z = (z.reshape(8, HID, WIDTH) + mixb_sc[...][None]).reshape(256, WIDTH)
            second = gelu_of_twice(z)
            o = jnp.dot(out_sc[...], second, preferred_element_type=F32)
            rows = slice(rb * 8, rb * 8 + 8)
            for c in range(2):
                out[t, c, rows, here] = o[c * 8:c * 8 + 8] + ob[0, c] - adj_sc[t, c, rows, here]


def shift_lanes(x, amount):
    return pltpu.roll(x.astype(F32), amount, 1).astype(BF16)


def kernel(n_lat, bg, sens, obs, de, dn, dk, cw, cb, mw, mb, ow, ob, out,
           xg_sc, e_sc, h_sc, halo_sc, call_sc, sens_sc, obs_sc,
           hx_sc, cf_sc, cnt_sc, os_sc, adj_sc, rh_sc, w_sc, mix_sc, mixb_sc, out_sc,
           loc, s_lat, r_lat, s_tm, r_tm, s_sl, r_sl, s_z, r_z, s_y, r_y, s_c, r_c):
    tm, lat = lax.axis_index("tm"), lax.axis_index("lat")
    z_hi = lax.rem(tm, 2)
    partner = tm + 1 - 2 * z_hi
    step_y = 2 - 4 * z_hi
    onward = lax.rem(tm + step_y + N_TM, N_TM)
    up, down = lax.rem(lat + 1, n_lat), lax.rem(lat + n_lat - 1, n_lat)
    from_partner = 2 - 2 * z_hi
    to_partner = 2 * z_hi

    def remote(src, dst, ss, rs, dev):
        return pltpu.make_async_remote_copy(src_ref=src, dst_ref=dst, send_sem=ss, recv_sem=rs, device_id=dev, device_id_type=MESH)

    own = pltpu.make_async_copy(bg, xg_sc.at[1], loc.at[0])
    own.start()
    own_sens = pltpu.make_async_copy(sens.at[pl.ds(2 * tm, 2)], sens_sc.at[1, tm], loc.at[1])
    own_sens.start()
    own_obs = pltpu.make_async_copy(obs.at[pl.ds(2 * tm, 2)], obs_sc.at[1, tm], loc.at[2])
    own_obs.start()
    for n, ref in enumerate((de, dn, dk)):
        val = ref[...] - (MID_K if n == 2 else 0.0)
        call_sc[tm, 1, n] = val[0:8].astype(BF16)
        call_sc[tm, 2, n] = val[8:16].astype(BF16)
    own.wait()
    half = LON // 2
    for e, row in ((0, 15), (1, 0)):
        rows = [xg_sc[1, f, c].astype(F32)[row:row + 1, :] for f in range(2) for c in range(2)]
        rows = [r[:, :half] for r in rows] + [r[:, half:] for r in rows]
        e_sc[e] = jnp.concatenate(rows, axis=0).astype(BF16)

    barrier = pltpu.get_barrier_semaphore()
    for d in range(1, N_TM):
        pl.semaphore_signal(barrier, inc=1, device_id=(lax.rem(tm + d, N_TM), lat), device_id_type=MESH)
    for other in (up, down):
        pl.semaphore_signal(barrier, inc=1, device_id=(tm, other), device_id_type=MESH)
    pl.semaphore_wait(barrier, N_TM + 1)

    lat_copies = []
    for n, (dev, q_src, q_dst, e, rows) in enumerate(((up, 2, 0, 0, 8), (down, 1, 3, 1, 0))):
        lat_copies.append((
            remote(call_sc.at[tm, q_src], call_sc.at[tm, q_dst], s_lat.at[n, 0], r_lat.at[n, 0], (tm, dev)),
            remote(e_sc.at[e], h_sc.at[1, e], s_lat.at[n, 1], r_lat.at[n, 1], (tm, dev)),
            remote(bg.at[:, :, pl.ds(rows, 8), :], halo_sc.at[n], s_lat.at[n, 2], r_lat.at[n, 2], (tm, dev)),
        ))
    for m in range(2):
        for copies in lat_copies:
            copies[m].start()
    tm_copies = []
    for d in range(1, N_TM):
        to = lax.rem(tm + d, N_TM)
        for m, (src, dst) in enumerate(((sens, sens_sc), (obs, obs_sc))):
            cp = remote(src.at[pl.ds(2 * to, 2)], dst.at[1, tm], s_tm.at[m, d - 1], r_tm.at[m, d - 1], (to, lat))
            cp.start()
            tm_copies.append(cp)
    frames = []
    for n in range(CHUNKS):
        lanes = pl.ds(n * WIDTH, WIDTH)
        frames.append(remote(bg.at[:, :, :, lanes], xg_sc.at[to_partner, :, :, :, lanes], s_z.at[n], r_z.at[n], (partner, lat)))
    for n in range(2):
        frames[n].start()
    for copies in lat_copies:
        copies[2].start()

    for copies in lat_copies:
        copies[0].wait_recv()
    coef_z = remote(call_sc.at[tm], call_sc.at[tm], s_c.at[0], r_c.at[0], (partner, lat))
    coef_z.start()
    for copies in lat_copies:
        copies[1].wait_recv()
    edge_z = remote(h_sc.at[1], h_sc.at[to_partner], s_z.at[CHUNKS], r_z.at[CHUNKS], (partner, lat))
    edge_z.start()
    for n in range(2, CHUNKS):
        frames[n].start()

    build_weights(tm, lat, n_lat, cw, cb, mw, mb, ow, w_sc, mix_sc, mixb_sc, out_sc)

    own_sens.wait()
    own_obs.wait()
    for d in range(1, N_TM):
        frm = lax.rem(tm - d + N_TM, N_TM)
        for m, (src, dst) in enumerate(((sens, sens_sc), (obs, obs_sc))):
            remote(src.at[pl.ds(0, 2)], dst.at[1, frm], s_tm.at[m, d - 1], r_tm.at[m, d - 1], (frm, lat)).wait_recv()
    sensor_copies = []
    for n, (dev, side) in enumerate(((up, 0), (down, 2))):
        for m, ref in enumerate((sens_sc, obs_sc)):
            cp = remote(ref.at[1], ref.at[side], s_sl.at[n, m], r_sl.at[n, m], (tm, dev))
            cp.start()
            sensor_copies.append(cp)

    forwards = []

    def forward(src, dst, n):
        cp = remote(src, dst, s_y.at[n], r_y.at[n], (onward, lat))
        cp.start()
        forwards.append(cp)

    for n in range(2):
        lanes = pl.ds(n * WIDTH, WIDTH)
        frames[n].wait_recv()
        forward(xg_sc.at[from_partner, :, :, :, lanes], xg_sc.at[to_partner, :, :, :, lanes], n)
    pltpu.make_async_remote_copy(src_ref=call_sc.at[partner], dst_ref=call_sc.at[partner], send_sem=s_c.at[0], recv_sem=r_c.at[0],
                                 device_id=(partner, lat), device_id_type=MESH).wait_recv()
    coef_y = []
    pair = pl.ds(tm - z_hi, 2)
    for d in range(1, 4):
        cp = remote(call_sc.at[pair], call_sc.at[pair], s_c.at[d], r_c.at[d], (lax.rem(tm + 2 * d, N_TM), lat))
        cp.start()
        coef_y.append(cp)
    edge_z.wait_recv()
    forward(h_sc.at[from_partner], h_sc.at[to_partner], CHUNKS)
    for n in range(2, CHUNKS):
        lanes = pl.ds(n * WIDTH, WIDTH)
        frames[n].wait_recv()
        forward(xg_sc.at[from_partner, :, :, :, lanes], xg_sc.at[to_partner, :, :, :, lanes], n)
    for cp in sensor_copies:
        cp.wait_recv()
    build_spread(sens_sc, obs_sc, cnt_sc, os_sc)
    for d in range(1, 4):
        there = pl.ds(lax.rem(tm - z_hi - 2 * d + N_TM, N_TM), 2)
        remote(call_sc.at[there], call_sc.at[there], s_c.at[d], r_c.at[d], (lax.rem(tm + 2 * d, N_TM), lat)).wait_recv()
    build_coefficients(lat, n_lat, call_sc, cf_sc)
    for copies in lat_copies:
        copies[2].wait_recv()
    likelihood(lat, n_lat, xg_sc, halo_sc, cf_sc, cnt_sc, os_sc, adj_sc)
    for cp in forwards:
        cp.wait_recv()
    build_edges(h_sc, hx_sc)

    def one_chunk(n, carry):
        score_chunk(n, xg_sc, hx_sc, rh_sc, w_sc, mix_sc, mixb_sc, out_sc, ob, adj_sc, out)
        return carry

    lax.fori_loop(0, CHUNKS, one_chunk, 0)

    for copies in lat_copies:
        for cp in copies:
            cp.wait_send()
    for cp in tm_copies + sensor_copies + frames + [edge_z, coef_z] + forwards + coef_y:
        cp.wait_send()


def solution(mesh):
    n_lat = mesh.shape["lat"]

    def shards(background, conv_weight, conv_bias, mix_weight, mix_bias, out_weight, out_bias,
               drift_east, drift_north, diffusivity, sensors, observations):
        vmem = pl.BlockSpec(memory_space=pltpu.VMEM)
        hbm = pl.BlockSpec(memory_space=pl.ANY)
        smem = pl.BlockSpec(memory_space=pltpu.SMEM)
        dma = pltpu.SemaphoreType.DMA
        scratch = [
            pltpu.VMEM((3, 2, 2, ROWS, LON), BF16),
            pltpu.VMEM((2, 8, LON // 2), BF16),
            pltpu.VMEM((3, 2, 8, LON // 2), BF16),
            pltpu.VMEM((2, 2, 2, 8, LON), BF16),
            pltpu.VMEM((N_TM, 4, 3, 8, TILE), BF16),
            pltpu.VMEM((3, N_TM, 2, 1, 1, 128), I32),
            pltpu.VMEM((3, N_TM, 2, 1, 1, 2, 128), F32),
            pltpu.VMEM((EXTRA, LON), BF16),
            pltpu.VMEM((5, 32, LON), F32),
            pltpu.VMEM((2, 32, LON), F32),
            pltpu.VMEM((2, 2, 32, LON), F32),
            pltpu.VMEM((2, 2, ROWS, LON), F32),
            pltpu.VMEM((3, 224, WIDTH), BF16),
            pltpu.VMEM((2, 3, ROWS * HID, KDIM), BF16),
            pltpu.VMEM((256, 256), BF16),
            pltpu.VMEM((HID, WIDTH), F32),
            pltpu.VMEM((16, 256), BF16),
            dma((3,)), dma((2, 3)), dma((2, 3)), dma((2, 7)), dma((2, 7)), dma((2, 2)), dma((2, 2)),
            dma((CHUNKS + 1,)), dma((CHUNKS + 1,)), dma((CHUNKS + 1,)), dma((CHUNKS + 1,)), dma((4,)), dma((4,)),
        ]
        return pl.pallas_call(
            functools.partial(kernel, n_lat),
            out_shape=jax.ShapeDtypeStruct((2, 2, ROWS, LON), F32),
            in_specs=[hbm, hbm, hbm] + [vmem] * 8 + [smem],
            out_specs=vmem,
            scratch_shapes=scratch,
            compiler_params=pltpu.CompilerParams(collective_id=0, has_side_effects=True, vmem_limit_bytes=56 * 1024 * 1024),
        )(background, sensors, observations, drift_east, drift_north, diffusivity,
          conv_weight, conv_bias.reshape(1, HID), mix_weight, mix_bias.reshape(1, HID), out_weight, out_bias.reshape(1, 2))

    placed = (P("tm", None, "lat", None), P(), P(), P(), P(), P(), P(), P("lat", "tm"), P("lat", "tm"), P("lat", "tm"),
              P(None, "lat", "tm", None), P(None, "lat", "tm", None, None))
    return jax.shard_map(shards, mesh=mesh, in_specs=placed, out_specs=P("tm", None, "lat", None), check_vma=False)
```

profile of v0, /device:TPU:1, one launch (start us, length us, event | category | flops | bytes accessed | tf_op | source)
XLA Modules:
  0.0 62.3 jit_solution(7246004675380742492)
XLA Ops:
  0.0 60.4 %shard_map.118 = f32[2,2,16,2048]{3,2,1,0:T(8,128)} custom-call(bf16[2,2,16,2048]{3,2,1,0:T(8,128)(2,1)} %bg.1, s32[16,1,1,128]{3,2,1,0:T(1,128)} %sens.1, f32[16,1,1,2,128]{4,3,2,1,0:T(2,128)} %obs.1, f32[16,256]{1,0:T(8,128)} %de.1, f32[16,256]{1,0:T(8,128)} %dn.1, f32[16,256]{1,0:T(8,128)} %dk.1, bf16[32,90]{1,0:T(8,128)(2,1)} %cw.1, f32[1,32]{1,0:T(1,128)} %bitcast.3, ...), custom_call_target="tpu_custom_call" | custom-call | tf_op jit(solution)/shard_map/pallas_call | solution.py:385
  60.4 1.9 %copy.14 = f32[2,2,16,2048]{3,2,1,0:T(8,128)} copy(f32[2,2,16,2048]{3,2,1,0:T(8,128)} %shard_map.118) | data formatting | bytes 1048576
where the time goes:
time: 62.5 us; the launch traced here: 62.3 us
  Pallas kernels  60.4 us (97%)
  local copies, waits for them, and re-layouts  1.87 us (3%)
    pallas_call x1, Pallas kernels, shards(): pl.pallas_call(functools.partial(kernel, n_lat), out_shape=jax.ShapeDtype...  60.4 us
    unnamed x1, local copies, waits for them, and re-layouts  1.87 us

commit v1 on v0

v1 whole, which is shorter than its diff:
```python
import functools

import jax
import jax.numpy as jnp
from jax import lax
from jax.experimental import pallas as pl
from jax.experimental.pallas import tpu as pltpu
from jax.sharding import PartitionSpec as P

MESH = pl.DeviceIdType.MESH
F32, BF16, I32 = jnp.float32, jnp.bfloat16, jnp.int32
N_TM = 8
ROWS, LON, TILE = 16, 2048, 256
HID, TAPS, KT, SUB = 32, 90, 5, 3
MID_K = 0.17
CHUNKS = 8
WIDTH = LON // CHUNKS
GELU_A = 1.5957691216057308
GELU_B = 0.2854192627
MAIN, EXTRA = 160, 32
KDIM = MAIN + EXTRA
PAD = 8
WINDOW = 3


def gelu_of_twice(y):
    t = jnp.tanh(y * (GELU_A + GELU_B * (y * y)))
    return (y + y * t).astype(BF16)


def iota(shape, dim):
    return lax.broadcasted_iota(I32, shape, dim)


def as_f32(mask):
    return jnp.where(mask, 1.0, 0.0).astype(F32)


def column(row):
    n = row.shape[1]
    eye = iota((n, n), 0) == iota((n, n), 1)
    return jnp.sum(jnp.where(eye, jnp.broadcast_to(row, (n, n)), 0.0), axis=1, keepdims=True)


def build_weights(tm, lat, n_lat, cw, cb, mw, mb, ow, w_sc, mix_sc, mixb_sc, out_sc):
    half_cw = (cw[...].astype(F32) * 0.5).astype(BF16)
    bias = column(cb[...] * 0.5)
    bias_hi = bias.astype(BF16).astype(F32)
    bias_lo = bias - bias_hi
    k = iota((1, KDIM), 1)
    main = k < MAIN
    kk = k - MAIN
    group_h, edge, f_h = kk // 8, (kk // 4) % 2, (kk // 2) % 2
    c = jnp.where(main, (k // 16) % 2, kk % 2)
    row_in = k % 16
    has_prev, has_next = tm > 0, tm < N_TM - 1
    has_south, has_north = lat > 0, lat < n_lat - 1
    bias_row = (as_f32(k == MAIN + 24) * bias_hi + as_f32(k == MAIN + 25) * bias_lo).astype(BF16)
    expanded = {}
    for t in range(2):
        lag = jnp.where(main, k // 32, 2 * group_h + f_h - t)
        group = (lag + t) // 2
        ok = (lag >= 0) & (lag < KT) & (main | (kk < 24))
        ok = ok & ((group > 0) | has_prev) & ((group < 2) | has_next)
        offset = iota((TAPS, KDIM), 0) - jnp.where(ok, (c * KT + lag) * 9, 1000)
        for j in range(3):
            for i in range(3):
                select = as_f32(offset == i * 3 + j).astype(BF16)
                expanded[t, j, i] = jnp.dot(half_cw, select, preferred_element_type=F32).astype(BF16)

    def one_row(r, carry):
        spot = [as_f32(main & (row_in == r + i - 1)) for i in range(3)]
        spot[0] = spot[0] + as_f32((~main) & (edge == 0) & (r == 0) & has_south)
        spot[2] = spot[2] + as_f32((~main) & (edge == 1) & (r == ROWS - 1) & has_north)
        spot = [jnp.broadcast_to(p, (HID, KDIM)).astype(BF16) for p in spot]
        for t in range(2):
            for j in range(3):
                val = expanded[t, j, 0] * spot[0] + expanded[t, j, 1] * spot[1] + expanded[t, j, 2] * spot[2]
                if j == 1:
                    val = val + bias_row
                w_sc[t, j, pl.ds(pl.multiple_of(r * HID, HID), HID), :] = val
        return carry

    lax.fori_loop(0, ROWS, one_row, 0)
    spread_lanes = as_f32(iota((HID, 8 * HID), 1) % HID == iota((HID, 8 * HID), 0)).astype(BF16)
    lane_row = iota((1, 8 * HID), 1) // HID
    mix_wide = jnp.dot((mw[...].astype(F32) * 0.5).astype(BF16), spread_lanes, preferred_element_type=F32)
    for r in range(8):
        mix_sc[r * HID:(r + 1) * HID, :] = (mix_wide * as_f32(lane_row == r)).astype(BF16)
    mixb_sc[...] = jnp.broadcast_to(column(mb[...] * 0.5), (HID, WIDTH))
    out_wide = jnp.dot(ow[...], spread_lanes, preferred_element_type=F32)
    own_row = iota((16, 8 * HID), 1) // HID == iota((16, 8 * HID), 0) % 8
    first_var = iota((16, 8 * HID), 0) < 8
    both = jnp.where(first_var, jnp.broadcast_to(out_wide[0:1], (16, 8 * HID)), jnp.broadcast_to(out_wide[1:2], (16, 8 * HID)))
    out_sc[...] = jnp.where(own_row, both, 0.0).astype(BF16)


def build_edges(h_sc, hx_sc):
    half = LON // 2
    for hf in range(2):
        parts = []
        for g in range(3):
            for e in range(2):
                parts.append(h_sc[g, e].astype(F32)[hf * 4:hf * 4 + 4, :])
        tail = as_f32(iota((8, half), 0) < 2)
        hx_sc[:, hf * half:(hf + 1) * half] = jnp.concatenate(parts + [tail], axis=0).astype(BF16)


def build_coefficients(lat, n_lat, call_sc, cf_sc, fields):
    for ref in fields[0] + fields[1]:
        for j in range(LON // 128):
            ref[j, 0:PAD, :] = jnp.zeros((PAD, 128), F32)
            ref[j, PAD + 32:, :] = jnp.zeros((PAD, 128), F32)
    lane = iota((32, 128), 1)
    live = jnp.where(lat > 0, 1.0, 0.0), jnp.where(lat < n_lat - 1, 1.0, 0.0)
    inside = jnp.concatenate([jnp.full((8, 128), live[0], F32), jnp.ones((16, 128), F32), jnp.full((8, 128), live[1], F32)], axis=0)

    def one_tile(j, carry):
        tile, lanes = j // 2, pl.ds(pl.multiple_of(lax.rem(j, 2) * 128, 128), 128)
        a, b, k = (jnp.concatenate([call_sc[tile, q, n, :, lanes].astype(F32) for q in range(4)], axis=0) for n in range(3))
        k = (k + MID_K) * inside
        a = a * (inside * 0.5)
        b = b * (inside * 0.5)
        center = inside - 4.0 * k
        cf_sc[0, 0, j] = center
        cf_sc[0, 1, j] = k - a
        cf_sc[0, 2, j] = k + a
        cf_sc[0, 3, j] = k - b
        cf_sc[0, 4, j] = k + b
        cf_sc[1, 0, j] = center
        cf_sc[1, 3, j] = pltpu.roll(k + b, 31, 0)
        cf_sc[1, 4, j] = pltpu.roll(k - b, 1, 0)
        return carry

    lax.fori_loop(0, LON // 128, one_tile, 0)

    def shifted(j, carry):
        tiles = LON // 128
        after, before = lax.rem(j + 1, tiles), lax.rem(j + tiles - 1, tiles)
        cf_sc[1, 1, j] = jnp.where(lane == 127, pltpu.roll(cf_sc[0, 2, after], 127, 1), pltpu.roll(cf_sc[0, 2, j], 127, 1))
        cf_sc[1, 2, j] = jnp.where(lane == 0, pltpu.roll(cf_sc[0, 1, before], 1, 1), pltpu.roll(cf_sc[0, 1, j], 1, 1))
        return carry

    lax.fori_loop(0, LON // 128, shifted, 0)


def build_spread(sens_sc, obs_sc, cnt_sc, os_sc):
    col = iota((TILE, 128), 0)
    sides = ((0, 8, 0, 8), (1, 16, 8, 0), (2, 8, 24, 0))

    def one(tile, carry):
        for f in range(2):
            for side, count, at, first_row in sides:
                cell = sens_sc[side, tile, f, 0]
                there = lax.shift_right_logical(cell, 8) - first_row
                pick = as_f32(jnp.broadcast_to(there, (count, 128)) == iota((count, 128), 0))
                value = obs_sc[side, tile, f, 0, 0]
                high = value.astype(BF16).astype(F32)
                low = value - high
                left = jnp.concatenate([pick, pick * high[0:1], pick * high[1:2], pick * low[0:1], pick * low[1:2]], axis=0).astype(BF16)
                right = as_f32(jnp.broadcast_to(cell & (TILE - 1), (TILE, 128)) == col).astype(BF16)
                total = lax.dot_general(left, right, (((1,), (1,)), ((), ())), preferred_element_type=F32)
                rows = slice(at, at + count)
                for h in range(2):
                    part = total[:, lanes_of(h)]
                    cnt_sc[f, 2 * tile + h, rows, :] = part[0:count]
                    os_sc[f, 0, 2 * tile + h, rows, :] = part[count:2 * count] + part[3 * count:4 * count]
                    os_sc[f, 1, 2 * tile + h, rows, :] = part[2 * count:3 * count] + part[4 * count:5 * count]
        return carry

    lax.fori_loop(0, N_TM, one, 0)


def lanes_of(tile):
    return slice(tile * 128, tile * 128 + 128)


def model_step(src, load, store, cf_sc, which):
    tiles = LON // 128
    lane = iota((32, 128), 1)
    at_first, at_last = lane == 0, lane == 127

    def ready(j):
        u = load(j)
        return u, pltpu.roll(u, 1, 1), pltpu.roll(u, 127, 1)

    before = ready(tiles - 1)
    first = now = ready(0)
    for j in range(tiles):
        after = first if j == tiles - 1 else ready(j + 1)
        lower = jnp.where(at_first, before[1], now[1])
        higher = jnp.where(at_last, after[2], now[2])
        cf = cf_sc.at[which]
        new = (cf[0, j] * now[0] + cf[1, j] * higher + cf[2, j] * lower
               + cf[3, j] * src[j, PAD + 1:PAD + 33, :] + cf[4, j] * src[j, PAD - 1:PAD + 31, :])
        store(j, new)
        before, now = now, after


def likelihood(f, lat, n_lat, xg_sc, halo_sc, cf_sc, cnt_sc, os_sc, fields, adj_sc):
    south = jnp.where(lat > 0, 1.0, 0.0).astype(F32)
    north = jnp.where(lat < n_lat - 1, 1.0, 0.0).astype(F32)
    for c in range(2):
        for j in range(LON // 128):
            here = lanes_of(j)
            ref = fields[c][1]
            ref[j, PAD:PAD + 8, :] = halo_sc[0, f, c, :, here].astype(F32) * south
            ref[j, PAD + 8:PAD + 24, :] = xg_sc[1, f, c, :, here].astype(F32)
            ref[j, PAD + 24:PAD + 32, :] = halo_sc[1, f, c, :, here].astype(F32) * north

    def store_to(ref, c, step):
        def store(j, new):
            if step == SUB - 1:
                ref[j, PAD:PAD + 32, :] = cnt_sc[f, j] * new - os_sc[f, c, j]
            elif step == 2 * SUB - 1:
                adj_sc[f, c, :, lanes_of(j)] = new[8:24]
            else:
                ref[j, PAD:PAD + 32, :] = new
        return store

    for step in range(2 * SUB):
        for c in range(2):
            src, dst = fields[c][1 - step % 2], fields[c][step % 2]
            model_step(src, lambda j: src[j, PAD:PAD + 32, :], store_to(dst, c, step), cf_sc, step // SUB)


def first_sums(n, xg_sc, hx_sc, rh_sc, w_sc, y_sc):
    base = pl.multiple_of(n * WIDTH, WIDTH)
    before = pl.multiple_of(lax.rem(n * WIDTH + LON - 128, LON), 128)
    after = pl.multiple_of(lax.rem(n * WIDTH + WIDTH, LON), 128)
    here = pl.ds(base, WIDTH)
    for piece in range(14):
        if piece < 12:
            g, f, c = piece // 4, (piece // 2) % 2, piece % 2
            load = lambda lanes: xg_sc[g, f, c, :, lanes]
        else:
            load = lambda lanes: hx_sc[(piece - 12) * 16:(piece - 11) * 16, lanes]
        rows = slice(piece * 16, piece * 16 + 16)
        mid = load(here)
        prev, nxt = load(pl.ds(before, 128)), load(pl.ds(after, 128))
        rh_sc[0, rows, :] = shift_lanes(jnp.concatenate([prev, mid], axis=1), 1)[:, 128:]
        rh_sc[1, rows, :] = mid
        rh_sc[2, rows, :] = shift_lanes(jnp.concatenate([mid, nxt], axis=1), WIDTH + 127)[:, :WIDTH]


def first_part(t, rh_sc, w_sc, y_sc):
    y = None
    for j in range(3):
        rhs = jnp.concatenate([rh_sc[j, t * 32:t * 32 + MAIN, :], rh_sc[j, 192:224, :]], axis=0)
        part = jnp.dot(w_sc[t, j], rhs, preferred_element_type=F32)
        y = part if y is None else y + part
    y_sc[t] = y


def finish_part(t, rb, n, y_sc, mix_sc, mixb_sc, out_sc, ob, adj_sc, out):
    here = pl.ds(pl.multiple_of(n * WIDTH, WIDTH), WIDTH)
    first = gelu_of_twice(y_sc[t, rb * 256:(rb + 1) * 256, :])
    z = jnp.dot(mix_sc[...], first, preferred_element_type=F32)
    z = (z.reshape(8, HID, WIDTH) + mixb_sc[...][None]).reshape(256, WIDTH)
    second = gelu_of_twice(z)
    o = jnp.dot(out_sc[...], second, preferred_element_type=F32)
    rows = slice(rb * 8, rb * 8 + 8)
    for c in range(2):
        out[t, c, rows, here] = o[c * 8:c * 8 + 8] + ob[0, c] - adj_sc[t, c, rows, here]


def shift_lanes(x, amount):
    return pltpu.roll(x, amount, 1)


def kernel(n_lat, bg, sens, obs, de, dn, dk, cw, cb, mw, mb, ow, ob, out,
           xg_sc, e_sc, h_sc, halo_sc, call_sc, sens_sc, obs_sc,
           hx_sc, cf_sc, cnt_sc, os_sc, adj_sc, ua_sc, ub_sc, uc_sc, ud_sc, rh_sc, y_sc, y2_sc, w_sc, mix_sc, mixb_sc, out_sc,
           loc, s_lat, r_lat, s_e, r_e, s_h, r_h, s_tm, r_tm, s_sl, r_sl, s_z, r_z, s_y, r_y, s_c, r_c):
    tm, lat = lax.axis_index("tm"), lax.axis_index("lat")
    z_hi = lax.rem(tm, 2)
    partner = tm + 1 - 2 * z_hi
    step_y = 2 - 4 * z_hi
    onward = lax.rem(tm + step_y + N_TM, N_TM)
    up, down = lax.rem(lat + 1, n_lat), lax.rem(lat + n_lat - 1, n_lat)
    from_partner = 2 - 2 * z_hi
    to_partner = 2 * z_hi

    def remote(src, dst, ss, rs, dev):
        return pltpu.make_async_remote_copy(src_ref=src, dst_ref=dst, send_sem=ss, recv_sem=rs, device_id=dev, device_id_type=MESH)

    own = pltpu.make_async_copy(bg, xg_sc.at[1], loc.at[0])
    own.start()
    own_sens = pltpu.make_async_copy(sens.at[pl.ds(2 * tm, 2)], sens_sc.at[1, tm], loc.at[1])
    own_sens.start()
    own_obs = pltpu.make_async_copy(obs.at[pl.ds(2 * tm, 2)], obs_sc.at[1, tm], loc.at[2])
    own_obs.start()
    for n, ref in enumerate((de, dn, dk)):
        val = ref[...] - (MID_K if n == 2 else 0.0)
        call_sc[tm, 1, n] = val[0:8].astype(BF16)
        call_sc[tm, 2, n] = val[8:16].astype(BF16)
    own.wait()
    half = LON // 2
    for e, row in ((0, 15), (1, 0)):
        rows = [xg_sc[1, f, c].astype(F32)[row:row + 1, :] for f in range(2) for c in range(2)]
        rows = [r[:, :half] for r in rows] + [r[:, half:] for r in rows]
        e_sc[e] = jnp.concatenate(rows, axis=0).astype(BF16)

    barrier = pltpu.get_barrier_semaphore()
    for d in range(1, N_TM):
        pl.semaphore_signal(barrier, inc=1, device_id=(lax.rem(tm + d, N_TM), lat), device_id_type=MESH)
    for other in (up, down):
        for who in (tm, partner):
            pl.semaphore_signal(barrier, inc=1, device_id=(who, other), device_id_type=MESH)
    build_weights(tm, lat, n_lat, cw, cb, mw, mb, ow, w_sc, mix_sc, mixb_sc, out_sc)
    pl.semaphore_wait(barrier, N_TM + 3)

    near = []
    for n, (dev, q_src, q_dst, e) in enumerate(((up, 2, 0, 0), (down, 1, 3, 1))):
        for w, (who, slot) in enumerate(((tm, 1), (partner, to_partner))):
            near.append(remote(call_sc.at[tm, q_src], call_sc.at[tm, q_dst], s_lat.at[n, w], r_lat.at[n, w], (who, dev)))
            near.append(remote(e_sc.at[e], h_sc.at[slot, e], s_e.at[n, w], r_e.at[n, w], (who, dev)))
    coef_z = remote(call_sc.at[tm, pl.ds(1, 2)], call_sc.at[tm, pl.ds(1, 2)], s_c.at[0], r_c.at[0], (partner, lat))
    coef_z.start()
    for cp in near:
        cp.start()
    tm_copies = []
    for d in range(1, N_TM):
        to = lax.rem(tm + d, N_TM)
        for m, (src, dst) in enumerate(((sens, sens_sc), (obs, obs_sc))):
            cp = remote(src.at[pl.ds(2 * to, 2)], dst.at[1, tm], s_tm.at[m, d - 1], r_tm.at[m, d - 1], (to, lat))
            cp.start()
            tm_copies.append(cp)
    halos = []
    for n, (dev, rows) in enumerate(((up, 8), (down, 0))):
        halos.append(remote(bg.at[:, :, pl.ds(rows, 8), :], halo_sc.at[n], s_h.at[n], r_h.at[n], (tm, dev)))
    frames = []
    for n in range(CHUNKS):
        lanes = pl.ds(n * WIDTH, WIDTH)
        frames.append(remote(bg.at[:, :, :, lanes], xg_sc.at[to_partner, :, :, :, lanes], s_z.at[n], r_z.at[n], (partner, lat)))
    order = [CHUNKS - 1] + list(range(CHUNKS - 1))
    for cp in halos + [frames[n] for n in order[:WINDOW]]:
        cp.start()

    def arrive(n):
        return remote(bg.at[:, :, :, pl.ds(0, WIDTH)], xg_sc.at[from_partner, :, :, :, lanes_at(n)], s_z.at[n], r_z.at[n], (partner, lat))

    def onto(n):
        return remote(xg_sc.at[from_partner, :, :, :, lanes_at(n)], xg_sc.at[to_partner, :, :, :, lanes_at(n)], s_y.at[n], r_y.at[n], (onward, lat))

    def relay(k):
        arrive(order[k]).wait_recv()
        onto(order[k]).start()
        if k + WINDOW < CHUNKS:
            frames[order[k + WINDOW]].start()

    for n, q_dst in enumerate((0, 3)):
        for w, who in enumerate((tm, partner)):
            there = call_sc.at[who, q_dst]
            remote(there, there, s_lat.at[n, w], r_lat.at[n, w], (partner, lat)).wait_recv()
    there = call_sc.at[partner, pl.ds(1, 2)]
    remote(there, there, s_c.at[0], r_c.at[0], (partner, lat)).wait_recv()
    coef_y = []
    pair = pl.ds(tm - z_hi, 2)
    for d in range(1, 4):
        cp = remote(call_sc.at[pair], call_sc.at[pair], s_c.at[d], r_c.at[d], (lax.rem(tm + 2 * d, N_TM), lat))
        cp.start()
        coef_y.append(cp)
    for n in range(2):
        for w, slot in enumerate((1, from_partner)):
            there = h_sc.at[slot, n]
            remote(there, there, s_e.at[n, w], r_e.at[n, w], (partner, lat)).wait_recv()
    edge_y = remote(h_sc.at[from_partner], h_sc.at[to_partner], s_y.at[CHUNKS], r_y.at[CHUNKS], (onward, lat))
    edge_y.start()
    relay(0)
    own_sens.wait()
    own_obs.wait()
    for d in range(1, N_TM):
        frm = lax.rem(tm - d + N_TM, N_TM)
        for m, (src, dst) in enumerate(((sens, sens_sc), (obs, obs_sc))):
            remote(src.at[pl.ds(0, 2)], dst.at[1, frm], s_tm.at[m, d - 1], r_tm.at[m, d - 1], (frm, lat)).wait_recv()
    sensor_copies = []
    for n, (dev, side) in enumerate(((up, 0), (down, 2))):
        for m, ref in enumerate((sens_sc, obs_sc)):
            cp = remote(ref.at[1], ref.at[side], s_sl.at[n, m], r_sl.at[n, m], (tm, dev))
            cp.start()
            sensor_copies.append(cp)
    relay(1)
    for cp in sensor_copies:
        cp.wait_recv()
    build_spread(sens_sc, obs_sc, cnt_sc, os_sc)
    relay(2)
    edge_y.wait_recv()
    build_edges(h_sc, hx_sc)
    relay(3)

    def conv_pairs(low, high):
        def two_chunks(m, carry):
            @pl.when(m == 1)
            def _():
                relay(7)
                onto(4).wait_recv()
                onto(5).wait_recv()

            @pl.when(m == 2)
            def _():
                onto(6).wait_recv()

            for odd in range(2):
                n = 2 * m + odd
                now, later = (y_sc, y2_sc) if odd == 0 else (y2_sc, y_sc)
                first_sums(jnp.minimum(n + 1, CHUNKS - 1), xg_sc, hx_sc, rh_sc, w_sc, later)
                for t in range(2):
                    first_part(t, rh_sc, w_sc, later)
                    for rb in range(2):
                        finish_part(t, rb, n, now, mix_sc, mixb_sc, out_sc, ob, adj_sc, out)
            return carry

        lax.fori_loop(low, high, two_chunks, 0)

    def conv_start():
        for n in order[:5]:
            onto(n).wait_recv()
        first_sums(0, xg_sc, hx_sc, rh_sc, w_sc, y_sc)
        for t in range(2):
            first_part(t, rh_sc, w_sc, y_sc)

    def finish_likelihood():
        for d in range(1, 4):
            there = pl.ds(lax.rem(tm - z_hi - 2 * d + N_TM, N_TM), 2)
            remote(call_sc.at[there], call_sc.at[there], s_c.at[d], r_c.at[d], (lax.rem(tm + 2 * d, N_TM), lat)).wait_recv()
        fields = ((ua_sc, ub_sc), (uc_sc, ud_sc))
        build_coefficients(lat, n_lat, call_sc, cf_sc, fields)
        for cp in halos:
            cp.wait_recv()

        def one_frame(f, carry):
            likelihood(f, lat, n_lat, xg_sc, halo_sc, cf_sc, cnt_sc, os_sc, fields, adj_sc)
            for n in range(2):
                @pl.when(f == n)
                def _():
                    relay(n + 4)
            return carry

        lax.fori_loop(0, 2, one_frame, 0)

    finish_likelihood()
    relay(6)
    conv_start()
    conv_pairs(0, CHUNKS // 2)

    for n in range(CHUNKS):
        onto(n).wait_send()
    for cp in near + halos + tm_copies + sensor_copies + frames + [coef_z, edge_y] + coef_y:
        cp.wait_send()


def lanes_at(n):
    return pl.ds(pl.multiple_of(n * WIDTH, WIDTH), WIDTH)


def solution(mesh):
    n_lat = mesh.shape["lat"]

    def shards(background, conv_weight, conv_bias, mix_weight, mix_bias, out_weight, out_bias,
               drift_east, drift_north, diffusivity, sensors, observations):
        vmem = pl.BlockSpec(memory_space=pltpu.VMEM)
        hbm = pl.BlockSpec(memory_space=pl.ANY)
        smem = pl.BlockSpec(memory_space=pltpu.SMEM)
        dma = pltpu.SemaphoreType.DMA
        scratch = [
            pltpu.VMEM((3, 2, 2, ROWS, LON), BF16),
            pltpu.VMEM((2, 8, LON // 2), BF16),
            pltpu.VMEM((3, 2, 8, LON // 2), BF16),
            pltpu.VMEM((2, 2, 2, 8, LON), BF16),
            pltpu.VMEM((N_TM, 4, 3, 8, TILE), BF16),
            pltpu.VMEM((3, N_TM, 2, 1, 1, 128), I32),
            pltpu.VMEM((3, N_TM, 2, 1, 1, 2, 128), F32),
            pltpu.VMEM((EXTRA, LON), BF16),
            pltpu.VMEM((2, 5, LON // 128, 32, 128), F32),
            pltpu.VMEM((2, LON // 128, 32, 128), F32),
            pltpu.VMEM((2, 2, LON // 128, 32, 128), F32),
            pltpu.VMEM((2, 2, ROWS, LON), F32),
            pltpu.VMEM((LON // 128, 32 + 2 * PAD, 128), F32),
            pltpu.VMEM((LON // 128, 32 + 2 * PAD, 128), F32),
            pltpu.VMEM((LON // 128, 32 + 2 * PAD, 128), F32),
            pltpu.VMEM((LON // 128, 32 + 2 * PAD, 128), F32),
            pltpu.VMEM((3, 224, WIDTH), BF16),
            pltpu.VMEM((2, ROWS * HID, WIDTH), F32),
            pltpu.VMEM((2, ROWS * HID, WIDTH), F32),
            pltpu.VMEM((2, 3, ROWS * HID, KDIM), BF16),
            pltpu.VMEM((256, 256), BF16),
            pltpu.VMEM((HID, WIDTH), F32),
            pltpu.VMEM((16, 256), BF16),
            dma((3,)), dma((2, 2)), dma((2, 2)), dma((2, 2)), dma((2, 2)), dma((2,)), dma((2,)), dma((2, 7)), dma((2, 7)), dma((2, 2)), dma((2, 2)),
            dma((CHUNKS + 1,)), dma((CHUNKS + 1,)), dma((CHUNKS + 1,)), dma((CHUNKS + 1,)), dma((4,)), dma((4,)),
        ]
        return pl.pallas_call(
            functools.partial(kernel, n_lat),
            out_shape=jax.ShapeDtypeStruct((2, 2, ROWS, LON), F32),
            in_specs=[hbm, hbm, hbm] + [vmem] * 8 + [smem],
            out_specs=vmem,
            scratch_shapes=scratch,
            compiler_params=pltpu.CompilerParams(collective_id=0, has_side_effects=True, vmem_limit_bytes=56 * 1024 * 1024),
        )(background, sensors, observations, drift_east, drift_north, diffusivity,
          conv_weight, conv_bias.reshape(1, HID), mix_weight, mix_bias.reshape(1, HID), out_weight, out_bias.reshape(1, 2))

    placed = (P("tm", None, "lat", None), P(), P(), P(), P(), P(), P(), P("lat", "tm"), P("lat", "tm"), P("lat", "tm"),
              P(None, "lat", "tm", None), P(None, "lat", "tm", None, None))
    return jax.shard_map(shards, mesh=mesh, in_specs=placed, out_specs=P("tm", None, "lat", None), check_vma=False)
```

time: 62.5 us -> 51.1 us (0.82)
  the two profiles are of different devices: /device:TPU:1 before, /device:TPU:2 now
where the time goes in v1:
time: 51.1 us; the launch traced here: 50.9 us
  Pallas kernels  49 us (96%)
  local copies, waits for them, and re-layouts  1.87 us (4%)
    pallas_call x1, Pallas kernels, shards(): pl.pallas_call(functools.partial(kernel, n_lat), out_shape=jax.ShapeDtype...  49 us
    unnamed x1, local copies, waits for them, and re-layouts  1.87 us

profile of v1, /device:TPU:2, one launch (start us, length us, event | category | flops | bytes accessed | tf_op | source)
XLA Modules:
  0.0 50.9 jit_solution(13545550398212960992)
XLA Ops:
  0.0 49.0 %shard_map.118 = f32[2,2,16,2048]{3,2,1,0:T(8,128)} custom-call(bf16[2,2,16,2048]{3,2,1,0:T(8,128)(2,1)} %bg.1, s32[16,1,1,128]{3,2,1,0:T(1,128)} %sens.1, f32[16,1,1,2,128]{4,3,2,1,0:T(2,128)} %obs.1, f32[16,256]{1,0:T(8,128)} %de.1, f32[16,256]{1,0:T(8,128)} %dn.1, f32[16,256]{1,0:T(8,128)} %dk.1, bf16[32,90]{1,0:T(8,128)(2,1)} %cw.1, f32[1,32]{1,0:T(1,128)} %bitcast.3, ...), custom_call_target="tpu_custom_call" | custom-call | tf_op jit(solution)/shard_map/pallas_call | solution.py:493
  49.1 1.9 %copy.14 = f32[2,2,16,2048]{3,2,1,0:T(8,128)} copy(f32[2,2,16,2048]{3,2,1,0:T(8,128)} %shard_map.118) | data formatting | bytes 1048576

commit v2 on v1

--- a/solution.py
+++ b/solution.py
@@ -20,7 +20,7 @@
 MAIN, EXTRA = 160, 32
 KDIM = MAIN + EXTRA
 PAD = 8
-WINDOW = 3
+WINDOW = 4
 
 
 def gelu_of_twice(y):
@@ -334,8 +334,8 @@
         lanes = pl.ds(n * WIDTH, WIDTH)
         frames.append(remote(bg.at[:, :, :, lanes], xg_sc.at[to_partner, :, :, :, lanes], s_z.at[n], r_z.at[n], (partner, lat)))
     order = [CHUNKS - 1] + list(range(CHUNKS - 1))
-    for cp in halos + [frames[n] for n in order[:WINDOW]]:
-        cp.start()
+    for n in order[:WINDOW]:
+        frames[n].start()
 
     def arrive(n):
         return remote(bg.at[:, :, :, pl.ds(0, WIDTH)], xg_sc.at[from_partner, :, :, :, lanes_at(n)], s_z.at[n], r_z.at[n], (partner, lat))
@@ -346,8 +346,6 @@
     def relay(k):
         arrive(order[k]).wait_recv()
         onto(order[k]).start()
-        if k + WINDOW < CHUNKS:
-            frames[order[k + WINDOW]].start()
 
     for n, q_dst in enumerate((0, 3)):
         for w, who in enumerate((tm, partner)):
@@ -380,14 +378,16 @@
             cp = remote(ref.at[1], ref.at[side], s_sl.at[n, m], r_sl.at[n, m], (tm, dev))
             cp.start()
             sensor_copies.append(cp)
+    for cp in halos + [frames[n] for n in order[WINDOW:]]:
+        cp.start()
     relay(1)
+    relay(2)
     for cp in sensor_copies:
         cp.wait_recv()
     build_spread(sens_sc, obs_sc, cnt_sc, os_sc)
-    relay(2)
+    relay(3)
     edge_y.wait_recv()
     build_edges(h_sc, hx_sc)
-    relay(3)
 
     def conv_pairs(low, high):
         def two_chunks(m, carry):

time: 51.1 us -> 48.8 us (0.955)
  the two profiles are of different devices: /device:TPU:2 before, /device:TPU:36 now
where the time goes in v2:
time: 48.8 us; the launch traced here: 48.7 us
  Pallas kernels  46.8 us (96%)
  local copies, waits for them, and re-layouts  1.87 us (4%)
    pallas_call x1, Pallas kernels, shards(): pl.pallas_call(functools.partial(kernel, n_lat), out_shape=jax.ShapeDtype...  46.8 us
    unnamed x1, local copies, waits for them, and re-layouts  1.87 us

profile of v2, /device:TPU:36, one launch (start us, length us, event | category | flops | bytes accessed | tf_op | source)
XLA Modules:
  0.0 48.7 jit_solution(4387623779972742034)
XLA Ops:
  0.0 46.8 %shard_map.118 = f32[2,2,16,2048]{3,2,1,0:T(8,128)} custom-call(bf16[2,2,16,2048]{3,2,1,0:T(8,128)(2,1)} %bg.1, s32[16,1,1,128]{3,2,1,0:T(1,128)} %sens.1, f32[16,1,1,2,128]{4,3,2,1,0:T(2,128)} %obs.1, f32[16,256]{1,0:T(8,128)} %de.1, f32[16,256]{1,0:T(8,128)} %dn.1, f32[16,256]{1,0:T(8,128)} %dk.1, bf16[32,90]{1,0:T(8,128)(2,1)} %cw.1, f32[1,32]{1,0:T(1,128)} %bitcast.3, ...), custom_call_target="tpu_custom_call" | custom-call | tf_op jit(solution)/shard_map/pallas_call | solution.py:493
  46.8 1.9 %copy.14 = f32[2,2,16,2048]{3,2,1,0:T(8,128)} copy(f32[2,2,16,2048]{3,2,1,0:T(8,128)} %shard_map.118) | data formatting | bytes 1048576

commit v3 on v2

--- a/solution.py
+++ b/solution.py
@@ -332,7 +332,7 @@
     frames = []
     for n in range(CHUNKS):
         lanes = pl.ds(n * WIDTH, WIDTH)
-        frames.append(remote(bg.at[:, :, :, lanes], xg_sc.at[to_partner, :, :, :, lanes], s_z.at[n], r_z.at[n], (partner, lat)))
+        frames.append(remote(xg_sc.at[1, :, :, :, lanes], xg_sc.at[to_partner, :, :, :, lanes], s_z.at[n], r_z.at[n], (partner, lat)))
     order = [CHUNKS - 1] + list(range(CHUNKS - 1))
     for n in order[:WINDOW]:
         frames[n].start()

time: 48.8 us -> 48.8 us (level)
  no operation moved by 1% of the time
where the time goes in v3:
time: 48.8 us; the launch traced here: 48.6 us
  Pallas kernels  46.8 us (96%)
  local copies, waits for them, and re-layouts  1.87 us (4%)
    pallas_call x1, Pallas kernels, shards(): pl.pallas_call(functools.partial(kernel, n_lat), out_shape=jax.ShapeDtype...  46.8 us
    unnamed x1, local copies, waits for them, and re-layouts  1.87 us

profile of v3, /device:TPU:36, one launch (start us, length us, event | category | flops | bytes accessed | tf_op | source)
XLA Modules:
  0.0 48.6 jit_solution(8966377071599545077)
XLA Ops:
  0.0 46.8 %shard_map.118 = f32[2,2,16,2048]{3,2,1,0:T(8,128)} custom-call(bf16[2,2,16,2048]{3,2,1,0:T(8,128)(2,1)} %bg.1, s32[16,1,1,128]{3,2,1,0:T(1,128)} %sens.1, f32[16,1,1,2,128]{4,3,2,1,0:T(2,128)} %obs.1, f32[16,256]{1,0:T(8,128)} %de.1, f32[16,256]{1,0:T(8,128)} %dn.1, f32[16,256]{1,0:T(8,128)} %dk.1, bf16[32,90]{1,0:T(8,128)(2,1)} %cw.1, f32[1,32]{1,0:T(1,128)} %bitcast.3, ...), custom_call_target="tpu_custom_call" | custom-call | tf_op jit(solution)/shard_map/pallas_call | solution.py:493
  46.8 1.9 %copy.14 = f32[2,2,16,2048]{3,2,1,0:T(8,128)} copy(f32[2,2,16,2048]{3,2,1,0:T(8,128)} %shard_map.118) | data formatting | bytes 1048576
